TPU v7x, 512 devices: a whole 4x4x16 slice. The times are simulated.
512 devices in a mesh: freq: 64 (over z, x_hi, core), space: 8 (over x_lo, y).
Axes of the slice: x: 4 (x_hi: 2, x_lo: 2; x = x_hi * 2 + x_lo), y: 4, z: 16, core: 2. Of those that a mesh axis runs over, the one named last changes fastest.
Arguments:
- series: bfloat16 [2048, 131072], P('freq', 'space')
- starts: int32 [7], replicated, may hold values from 0 to 1536, as said below
- freqs: int32 [64], replicated, may hold values from 0 to 511, as said below
- alpha: int32 [1], replicated, may hold values from 1 to 63
Outputs:
- spectra: bfloat16 [64, 2, 7, 131072], P('freq', None, None, 'space')
- gram: float32 [64, 2, 63, 63], P('freq')
Inputs may be any that keep to these rules, and one draw needn't show every extreme that they name: `starts`: increasing; the first is 0, the last 1536; consecutive ones lie 512 / 4 to 384 apart. `freqs`: 64 distinct bins, 0 and 511 among them.
All inputs are finite; a program needn't handle non-finite values.
Results may differ from a plain program's by a relative error of at most 0.005.
Values may be sent and summed in bfloat16 or wider, within the bound.
No kernel may reach another device: no remote copies, remote signals or barrier semaphores. Data moves between devices by JAX's collectives and lax.ppermute only.
A program may use at most 64 MiB of HBM per device.

v0:
```python
import math
import jax
import jax.numpy as jnp
from jax import lax
from jax.sharding import PartitionSpec as P

NFFT = 512
NBLK = 7
HALF = 4
SHIFTS = 9


def transform_table(freqs, alpha):
    sample_index = jnp.arange(NFFT, dtype=jnp.int32)
    shift_index = jnp.arange(SHIFTS, dtype=jnp.int32) - HALF
    freq_bins = jnp.mod(freqs[:, None] + shift_index[None, :] * alpha[0], NFFT)
    phase_steps = jnp.mod(freq_bins[:, :, None] * sample_index[None, None, :], NFFT)
    phase = phase_steps.astype(jnp.float32) * (2.0 * math.pi / NFFT)
    sample_float = sample_index.astype(jnp.float32)
    window_shape = 0.5 - 0.5 * jnp.cos(sample_float * (2.0 * math.pi / NFFT))
    window_scale = window_shape / jnp.sqrt(jnp.sum(window_shape * window_shape))
    real_part = window_scale * jnp.cos(phase)
    imag_part = -(window_scale * jnp.sin(phase))
    return jnp.stack([real_part, imag_part], axis=1).astype(jnp.bfloat16)


def split_quadrants(products, order):
    real_gram = products[..., :order, :order] + products[..., order:, order:]
    imag_gram = products[..., :order, order:] - products[..., order:, :order]
    return jnp.stack([real_gram, imag_gram], axis=-3)


def per_device(series, starts, freqs, alpha):
    slab_cells = series.shape[1]
    total_cells = slab_cells * lax.axis_size("space")
    nfreq = freqs.shape[0]
    order = SHIFTS * NBLK
    local_rows = lax.all_to_all(series, "freq", split_axis=1, concat_axis=0, tiled=True)
    local_cells = local_rows.shape[1]
    flat_table = transform_table(freqs, alpha).reshape(nfreq * 2 * SHIFTS, NFFT)
    blocks = []
    for block in range(NBLK):
        block_rows = lax.dynamic_slice_in_dim(local_rows, starts[block], NFFT, 0)
        spec_block = jnp.dot(flat_table, block_rows, preferred_element_type=jnp.float32)
        blocks.append(spec_block.astype(jnp.bfloat16).reshape(nfreq, 2, SHIFTS, local_cells))
    blockspec = jnp.stack(blocks, axis=3)
    received = lax.all_to_all(blockspec, "freq", split_axis=0, concat_axis=4, tiled=True)
    stacked = received.reshape(2 * order, slab_cells)
    products = lax.dot_general(
        stacked, stacked, (((1,), (1,)), ((), ())), preferred_element_type=jnp.float32
    )
    gram_part = split_quadrants(products, order)[None]
    own_spectra = received[:, :, HALF]
    gram = lax.psum(gram_part, "space") / total_cells
    return (own_spectra, gram)


def solution(mesh):
    placed = (P("freq", "space"), P(), P(), P())
    return jax.shard_map(
        per_device,
        mesh=mesh,
        in_specs=placed,
        out_specs=(P("freq", None, None, "space"), P("freq", None, None, None)),
        check_vma=False,
    )
```

profile of v0, /device:TPU:4, one launch (start us, length us, event | category | flops | bytes accessed | tf_op | source)
XLA Modules:
  0.0 362.7 jit_solution(13131280645304690328)
XLA Ops:
  0.6 2.3 copy.29
  3.0 18.9 %all-to-all-start = ((bf16[32,64,256]{2,0,1:T(8,128)(2,1)}), bf16[32,64,256]{2,0,1:T(8,128)(2,1)}, u32[]{:S(2)}, u32[]{:S(2)}) async-start(bf16[32,64,256]{2,0,1:T(8,128)(2,1)} %bitcast.40), calls=%async_computation | async-start | bytes 2097152 | tf_op jit(solution)/shard_map/all_to_all | solution.py:38
  33.3 5.4 %multiply_convert_fusion = (bf16[64,1,9,512]{3,0,2,1:T(8,128)(2,1)S(1)}, bf16[64,1,9,512]{3,0,2,1:T(8,128)(2,1)S(1)}) fusion(s32[64,9]{0,1:T(8,128)S(1)} %add_select_fusion.2, f32[512]{0:T(512)S(1)} %fusion.16), kind=kLoop, calls=%fused_computation.15 | loop fusion | flops 5603328 | bytes 1184000 | tf_op jit(solution)/shard_map/convert
  44.5 33.4 %all-to-all-done = bf16[32,64,256]{2,0,1:T(8,128)(2,1)} async-done(((bf16[32,64,256]{2,0,1:T(8,128)(2,1)}), bf16[32,64,256]{2,0,1:T(8,128)(2,1)}, u32[]{:S(2)}, u32[]{:S(2)}) %all-to-all-start) | async-done | bytes 1048608 | tf_op jit(solution)/shard_map/all_to_all | solution.py:38
  77.9 1.5 convolution_convert_fusion.6
  79.6 1.0 constant_dynamic-update-slice_fusion.6
  80.6 1.5 convolution_convert_fusion.5
  82.3 2.3 convolution_convert_fusion.4
  84.7 1.3 stack_reshape.23
  86.0 2.3 convolution_convert_fusion.3
  88.3 2.2 stack_reshape.24
  90.5 2.3 convolution_convert_fusion.2
  92.8 2.1 stack_reshape.25
  94.9 2.3 convolution_convert_fusion.1
  97.2 2.1 stack_reshape.26
  99.3 2.3 convolution_convert_fusion
  101.6 1.3 stack_reshape.27
  102.9 1.1 constant_dynamic-update-slice_fusion.5
  104.0 1.1 constant_dynamic-update-slice_fusion.4
  105.6 1.0 constant_dynamic-update-slice_fusion.3
  107.2 1.0 constant_dynamic-update-slice_fusion.2
  108.8 1.1 constant_dynamic-update-slice_fusion.1
  109.9 1.1 constant_dynamic-update-slice_fusion
  110.9 8.5 %copy.21 = bf16[64,2,9,7,256]{4,1,3,2,0:T(2,128)(2,1)} copy(bf16[64,2,9,7,256]{4,2,1,0,3:T(8,128)(2,1)} %constant_dynamic-update-slice_fusion) | data formatting | bytes 8257536 | tf_op jit(solution)/shard_map/stack | solution.py:46
  119.4 193.4 %all_to_all.37 = bf16[64,2,9,7,256]{4,1,3,2,0:T(2,128)(2,1)S(1)} all-to-all(bf16[64,2,9,7,256]{4,1,3,2,0:T(2,128)(2,1)} %copy.21), channel_id=1, replica_groups=mesh['freq'=64,'space'=8] {'freq'}, dimensions={0} | all-to-all | bytes 8257536 | tf_op jit(solution)/shard_map/all_to_all | solution.py:47
  312.8 0.9 copy.23
  313.7 1.0 copy-done
  315.3 2.9 copy.27
  318.2 1.2 fusion.25
  319.6 34.6 %psum.7 = f32[1,2,63,63]{3,2,1,0:T(8,128)S(1)} all-reduce(f32[1,2,63,63]{3,2,1,0:T(8,128)S(1)} %maximum_bitcast_fusion), channel_id=1, replica_groups=mesh['freq'=64,'space'=8] {'space'}, use_global_device_ids=true, to_apply=%region_1.2 | all-reduce | flops 7938 | bytes 63504 | tf_op jit(solution)/shard_map/psum | solution.py:54
  354.9 6.7 %copy.26 = bf16[1,64,9,7,1,2,256]{6,5,1,4,3,2,0:T(2,128)(2,1)S(1)} copy(bf16[1,64,9,7,1,2,256]{6,5,4,3,2,1,0:T(2,128)(2,1)} %bitcast.44) | data formatting | bytes 8257536 | tf_op jit(solution)/shard_map/all_to_all | solution.py:47
  361.6 1.1 slice_bitcast_fusion
  (26 shorter events, 6.3 us)
Async XLA Ops:
  3.0 18.9 %copy-start.4 = (s32[7]{0:T(128)S(1)}, s32[7]{0:T(128)}, u32[]{:S(2)}) copy-start(s32[7]{0:T(128)} %param.5) | copy-start | bytes 88
  3.0 30.3 %copy-start.5 = (s32[64]{0:T(128)S(1)}, s32[64]{0:T(128)}, u32[]{:S(2)}) copy-start(s32[64]{0:T(128)} %param.6) | copy-start | bytes 772
  3.0 74.9 %all-to-all-start = ((bf16[32,64,256]{2,0,1:T(8,128)(2,1)}), bf16[32,64,256]{2,0,1:T(8,128)(2,1)}, u32[]{:S(2)}, u32[]{:S(2)}) async-start(bf16[32,64,256]{2,0,1:T(8,128)(2,1)} %bitcast.40), calls=%async_computation | async-start | bytes 2097152 | tf_op jit(solution)/shard_map/all_to_all | solution.py:38
  104.0 1.6 copy-start.1
  105.6 1.6 copy-start.2
  107.2 1.6 copy-start.3
  312.8 1.9 copy-start
where the time goes:
time: 364 us; the launch traced here: 363 us
  blocking collectives  228 us (63%)
  local copies, waits for them, and re-layouts  45.3 us (12%)
  waiting for transfers between devices  33.4 us (9%)
  starting transfers between devices  18.9 us (5%)
  matrix products  15.6 us (4%)
  between operations  15.1 us (4%)
  other arithmetic  6.35 us (2%)
    all_to_all x1, blocking collectives, per_device(): lax.all_to_all(blockspec, 'freq', split_axis=0, concat_axis=4, tiled=True)  193 us
    psum x1, blocking collectives, per_device(): gram = lax.psum(gram_part, 'space') / total_cells  34.6 us
    all_to_all x1, waiting for transfers between devices, per_device(): lax.all_to_all(series, 'freq', split_axis=1, concat_axis=0, tiled=True)  33.4 us
    another operation x9, local copies, waits for them, and re-layouts, per_device(): blockspec = jnp.stack(blocks, axis=3)  19.1 us
    all_to_all x1, starting transfers between devices, per_device(): lax.all_to_all(series, 'freq', split_axis=1, concat_axis=0, tiled=True)  18.9 us
    dot_general x7, matrix products, per_device(): jnp.dot(flat_table, block_rows, preferred_element_type=jnp.float32)  14.3 us
    unnamed x21, local copies, waits for them, and re-layouts  13.2 us
    all_to_all x2, local copies, waits for them, and re-layouts, per_device(): lax.all_to_all(blockspec, 'freq', split_axis=0, concat_axis=4, tiled=True)  7.57 us
  transfers between devices with their start and end apart: 1, of which 1 were waited for; matrix products, arithmetic and copies ran while one was open for 2% of the time, Pallas kernels for 0%

commit v1 on v0

--- a/solution.py
+++ b/solution.py
@@ -8,6 +8,11 @@
 NBLK = 7
 HALF = 4
 SHIFTS = 9
+
+
+def add_all(value, axis):
+    pieces = lax.all_gather(value, axis)
+    return jnp.sum(pieces, axis=0)
 
 
 def transform_table(freqs, alpha):
@@ -51,7 +56,7 @@
     )
     gram_part = split_quadrants(products, order)[None]
     own_spectra = received[:, :, HALF]
-    gram = lax.psum(gram_part, "space") / total_cells
+    gram = add_all(gram_part, "space") / total_cells
     return (own_spectra, gram)
 
 

time: 364 us -> 359 us (0.986)
  blocking collectives: 228 us -> 223 us
    psum x1 -> x0, blocking collectives: 34.6 us -> none  [per_device(): gram = lax.psum(gram_part, 'space') / total_cells]
    all_gather x0 -> x1, blocking collectives: none -> 29.4 us  [add_all(): pieces = lax.all_gather(value, axis)]
where the time goes in v1:
time: 359 us; the launch traced here: 358 us
  blocking collectives  223 us (62%)
  local copies, waits for them, and re-layouts  45.3 us (13%)
  waiting for transfers between devices  33.4 us (9%)
  starting transfers between devices  18.9 us (5%)
  matrix products  15.6 us (4%)
  between operations  15.1 us (4%)
  other arithmetic  6.4 us (2%)
    all_to_all x1, blocking collectives, per_device(): lax.all_to_all(blockspec, 'freq', split_axis=0, concat_axis=4, tiled=True)  193 us
    all_to_all x1, waiting for transfers between devices, per_device(): lax.all_to_all(series, 'freq', split_axis=1, concat_axis=0, tiled=True)  33.4 us
    all_gather x1, blocking collectives, add_all(): pieces = lax.all_gather(value, axis)  29.4 us
    another operation x9, local copies, waits for them, and re-layouts, per_device(): blockspec = jnp.stack(blocks, axis=3)  19.1 us
    all_to_all x1, starting transfers between devices, per_device(): lax.all_to_all(series, 'freq', split_axis=1, concat_axis=0, tiled=True)  18.9 us
    dot_general x7, matrix products, per_device(): jnp.dot(flat_table, block_rows, preferred_element_type=jnp.float32)  14.3 us
    unnamed x21, local copies, waits for them, and re-layouts  13.2 us
    all_to_all x2, local copies, waits for them, and re-layouts, per_device(): lax.all_to_all(blockspec, 'freq', split_axis=0, concat_axis=4, tiled=True)  7.57 us
  transfers between devices with their start and end apart: 1, of which 1 were waited for; matrix products, arithmetic and copies ran while one was open for 2% of the time, Pallas kernels for 0%

profile of v1, /device:TPU:4, one launch (start us, length us, event | category | flops | bytes accessed | tf_op | source)
XLA Modules:
  0.0 357.6 jit_solution(498715291686584251)
XLA Ops:
  0.6 2.3 copy.26
  3.0 18.9 %all-to-all-start = ((bf16[32,64,256]{2,0,1:T(8,128)(2,1)}), bf16[32,64,256]{2,0,1:T(8,128)(2,1)}, u32[]{:S(2)}, u32[]{:S(2)}) async-start(bf16[32,64,256]{2,0,1:T(8,128)(2,1)} %bitcast.41), calls=%async_computation | async-start | bytes 2097152 | tf_op jit(solution)/shard_map/all_to_all | solution.py:43
  33.3 5.4 %multiply_convert_fusion = (bf16[64,1,9,512]{3,0,2,1:T(8,128)(2,1)S(1)}, bf16[64,1,9,512]{3,0,2,1:T(8,128)(2,1)S(1)}) fusion(s32[64,9]{0,1:T(8,128)S(1)} %add_select_fusion.2, f32[512]{0:T(512)S(1)} %fusion.16), kind=kLoop, calls=%fused_computation.15 | loop fusion | flops 5603328 | bytes 1184000 | tf_op jit(solution)/shard_map/convert
  44.5 33.4 %all-to-all-done = bf16[32,64,256]{2,0,1:T(8,128)(2,1)} async-done(((bf16[32,64,256]{2,0,1:T(8,128)(2,1)}), bf16[32,64,256]{2,0,1:T(8,128)(2,1)}, u32[]{:S(2)}, u32[]{:S(2)}) %all-to-all-start) | async-done | bytes 1048608 | tf_op jit(solution)/shard_map/all_to_all | solution.py:43
  77.9 1.5 convolution_convert_fusion.6
  79.6 1.0 constant_dynamic-update-slice_fusion.6
  80.6 1.5 convolution_convert_fusion.5
  82.3 2.3 convolution_convert_fusion.4
  84.7 1.3 stack_reshape.23
  86.0 2.3 convolution_convert_fusion.3
  88.3 2.2 stack_reshape.24
  90.5 2.3 convolution_convert_fusion.2
  92.8 2.1 stack_reshape.25
  94.9 2.3 convolution_convert_fusion.1
  97.2 2.1 stack_reshape.26
  99.3 2.3 convolution_convert_fusion
  101.6 1.3 stack_reshape.27
  102.9 1.1 constant_dynamic-update-slice_fusion.5
  104.0 1.1 constant_dynamic-update-slice_fusion.4
  105.6 1.0 constant_dynamic-update-slice_fusion.3
  107.2 1.0 constant_dynamic-update-slice_fusion.2
  108.8 1.1 constant_dynamic-update-slice_fusion.1
  109.9 1.1 constant_dynamic-update-slice_fusion
  110.9 8.5 %copy.18 = bf16[64,2,9,7,256]{4,1,3,2,0:T(2,128)(2,1)} copy(bf16[64,2,9,7,256]{4,2,1,0,3:T(8,128)(2,1)} %constant_dynamic-update-slice_fusion) | data formatting | bytes 8257536 | tf_op jit(solution)/shard_map/stack | solution.py:51
  119.4 193.4 %all_to_all.37 = bf16[64,2,9,7,256]{4,1,3,2,0:T(2,128)(2,1)S(1)} all-to-all(bf16[64,2,9,7,256]{4,1,3,2,0:T(2,128)(2,1)} %copy.18), channel_id=1, replica_groups=mesh['freq'=64,'space'=8] {'freq'}, dimensions={0} | all-to-all | bytes 8257536 | tf_op jit(solution)/shard_map/all_to_all | solution.py:52
  312.8 0.9 copy.20
  313.7 1.0 copy-done
  315.3 2.9 copy.24
  318.2 1.2 fusion.25
  319.6 29.4 %all-gather = f32[16,63,63]{2,1,0:T(8,128)S(1)} all-gather(f32[2,63,63]{2,1,0:T(8,128)S(1)} %pad_maximum_fusion.1), channel_id=2, replica_groups=mesh['freq'=64,'space'=8] {'space'}, dimensions={0}, use_global_device_ids=true | all-gather | bytes 285768 | tf_op jit(solution)/shard_map/all_gather | solution.py:14
  349.8 6.7 %copy.23 = bf16[1,64,9,7,1,2,256]{6,5,1,4,3,2,0:T(2,128)(2,1)S(1)} copy(bf16[1,64,9,7,1,2,256]{6,5,4,3,2,1,0:T(2,128)(2,1)} %bitcast.45) | data formatting | bytes 8257536 | tf_op jit(solution)/shard_map/all_to_all | solution.py:52
  356.5 1.1 slice_bitcast_fusion
  (27 shorter events, 6.4 us)
Async XLA Ops:
  3.0 18.9 %copy-start.4 = (s32[7]{0:T(128)S(1)}, s32[7]{0:T(128)}, u32[]{:S(2)}) copy-start(s32[7]{0:T(128)} %param.5) | copy-start | bytes 88
  3.0 30.3 %copy-start.5 = (s32[64]{0:T(128)S(1)}, s32[64]{0:T(128)}, u32[]{:S(2)}) copy-start(s32[64]{0:T(128)} %param.6) | copy-start | bytes 772
  3.0 74.9 %all-to-all-start = ((bf16[32,64,256]{2,0,1:T(8,128)(2,1)}), bf16[32,64,256]{2,0,1:T(8,128)(2,1)}, u32[]{:S(2)}, u32[]{:S(2)}) async-start(bf16[32,64,256]{2,0,1:T(8,128)(2,1)} %bitcast.41), calls=%async_computation | async-start | bytes 2097152 | tf_op jit(solution)/shard_map/all_to_all | solution.py:43
  104.0 1.6 copy-start.1
  105.6 1.6 copy-start.2
  107.2 1.6 copy-start.3
  312.8 1.9 copy-start
